TPU v7x, 256 devices: a whole 4x4x8 slice. The times are simulated.
256 devices in a mesh: row: 8 (over z), col: 32 (over y, x, core).
Axes of the slice: x: 4, y: 4, z: 8, core: 2. Of those that a mesh axis runs over, the one named last changes fastest.
Arguments:
- panel_block: bfloat16 [28672, 1024], P(('row', 'col')), may hold values from -1.5 to 1.5
- diag_inverse: bfloat16 [2, 512, 512], replicated
- trailing: bfloat16 [28672, 28672], P('row', 'col'), may hold values from -6 to 6
Outputs:
- factor_panel: bfloat16 [28672, 1024], P(('row', 'col'))
- updated: bfloat16 [28672, 28672], P('row', 'col')
All inputs are finite; a program needn't handle non-finite values.
Results may differ from a plain program's by a relative error of at most 0.0054.
Values may be sent and summed in bfloat16 or wider, within the bound.
A program may use at most 128 MiB of HBM per device.

v0:
```python
import jax
import jax.numpy as jnp
from jax import lax
from jax.sharding import PartitionSpec as P

NB = 512
PANELS = 2


def sent_to_all(x, axis):
    peers = lax.axis_size(axis)
    return lax.all_to_all(jnp.broadcast_to(x[None], (peers, *x.shape)), axis, 0, 0, tiled=True)


def laid_out(pieces, dim):
    pieces = jnp.moveaxis(pieces, 0, dim)
    dims = pieces.shape
    return pieces.reshape(*dims[:dim], dims[dim] * dims[dim + 1], *dims[dim + 2 :])


def collect(x, axis, dim):
    pieces = sent_to_all(x, axis)
    return laid_out(pieces, dim)


def body(panel_block, diag_inverse, trailing):
    pieces = []
    for panel in range(PANELS):
        columns = panel_block[:, panel * NB : (panel + 1) * NB]
        pieces.append(
            jnp.dot(
                columns, jnp.tril(diag_inverse[panel]).T, preferred_element_type=jnp.float32
            ).astype(jnp.bfloat16)
        )
    factor = jnp.concatenate(pieces, axis=1)
    row_block = lax.all_gather(factor, "col", axis=0, tiled=True)
    product = lax.dot_general(
        row_block,
        collect(factor, "row", 0),
        (((1,), (1,)), ((), ())),
        preferred_element_type=jnp.float32,
    )
    updated = (trailing.astype(jnp.float32) - product).astype(jnp.bfloat16)
    return (factor, updated)


def solution(mesh):
    placed = (P(("row", "col"), None), P(), P("row", "col"))
    return jax.shard_map(
        body,
        mesh=mesh,
        in_specs=placed,
        out_specs=(P(("row", "col"), None), P("row", "col")),
        check_vma=False,
    )
```

profile of v0, /device:TPU:1, one launch (start us, length us, event | category | flops | bytes accessed | tf_op | source)
XLA Modules:
  0.0 91.9 jit_solution(386972775527290636)
XLA Ops:
  7.2 0.0 all-gather.2.cloned.1.call-start
  7.2 1.3 %fusion.1 = bf16[112,512]{1,0:T(8,128)(2,1)S(1)} fusion(bf16[2,512,512]{2,1,0:T(8,128)(2,1)} %param.4, bf16[112,1024]{1,0:T(8,128)(2,1)} %param.3), kind=kOutput, calls=%fused_computation.4 | convolution fusion | flops 59301888 | bytes 753664 | tf_op jit(solution)/shard_map/dot_general | solution.py:31
  8.6 1.3 %fusion = bf16[112,512]{1,0:T(8,128)(2,1)S(1)} fusion(bf16[2,512,512]{2,1,0:T(8,128)(2,1)} %param.4, bf16[112,1024]{1,0:T(8,128)(2,1)} %param.3), kind=kOutput, calls=%fused_computation.3 | convolution fusion | flops 59301888 | bytes 753664 | tf_op jit(solution)/shard_map/dot_general | solution.py:31
  9.9 0.7 pad_maximum_fusion
  10.6 0.0 all-gather.2.cloned.1.call-update
  10.6 1.2 %broadcast_in_dim.12 = bf16[8,112,1024]{2,1,0:T(8,128)(2,1)S(1)} broadcast(bf16[112,1024]{1,0:T(8,128)(2,1)} %pad_maximum_fusion), dimensions={1,2} | broadcast | bytes 2064384 | tf_op jit(solution)/shard_map/broadcast_in_dim | solution.py:12
  11.8 52.9 %all_to_all.5 = bf16[8,112,1024]{2,1,0:T(8,128)(2,1)S(1)} all-to-all(bf16[8,112,1024]{2,1,0:T(8,128)(2,1)S(1)} %broadcast_in_dim.12), channel_id=1, replica_groups=mesh['row'=8,'col'=32] {'row'}, dimensions={0} | all-to-all | bytes 3670016 | tf_op jit(solution)/shard_map/all_to_all | solution.py:12
  64.7 6.6 %all-gather.2.cloned.1.call-done = bf16[3584,1024]{1,0:T(8,128)(2,1)} async-done(((bf16[112,1024]{1,0:T(8,128)(2,1)}), bf16[3584,1024]{1,0:T(8,128)(2,1)}) %all-gather.2.cloned.1.call-update) | async-done | bytes 7340048 | tf_op jit(solution)/shard_map/all_gather | solution.py:36
  71.3 13.8 %subtract_convert_fusion = bf16[3584,896]{1,0:T(8,128)(2,1)} fusion(bf16[3584,896]{1,0:T(8,128)(2,1)} %param.5, bf16[3584,1024]{1,0:T(8,128)(2,1)} %all-gather.2.cloned.1.call-done, bf16[896,1024]{1,0:T(8,128)(2,1)S(1)} %bitcast.17), kind=kOutput, calls=%fused_computation | convolution fusion | flops 6586302464 | bytes 22020096 | tf_op jit(solution)/shard_map/dot_general | solution.py:37
Async XLA Ops:
  7.2 64.1 %all-gather.2.cloned.1.call-start = ((), (), s32[]{:S(2)}) async-start(), calls=%async_computation.1 | async-start | bytes 7569408 | tf_op jit(solution)/shard_map/all_gather | solution.py:36
Sparse Core Ops, SparseCore 0:
  11.1 60.0 all-gather.1
where the time goes:
time: 92.1 us; the launch traced here: 91.9 us
  blocking collectives  52.9 us (57%)
  matrix products  16.5 us (18%)
  between operations  14 us (15%)
  waiting for transfers between devices  6.57 us (7%)
  local copies, waits for them, and re-layouts  1.16 us (1%)
    all_to_all x1, blocking collectives, sent_to_all(): lax.all_to_all(jnp.broadcast_to(x[None], (peers, *x.shape)), axis, 0, 0,...  52.9 us
    dot_general x1, matrix products, body(): lax.dot_general(row_block, collect(factor, 'row', 0), (((1,), (1,)), ((),...  13.8 us
    all_gather x1, waiting for transfers between devices, body(): row_block = lax.all_gather(factor, 'col', axis=0, tiled=True)  6.55 us
    dot_general x2, matrix products, body(): jnp.dot(columns, jnp.tril(diag_inverse[panel]).T, preferred_element_type=...  2.68 us
  transfers between devices with their start and end apart: 1, of which 1 were waited for; matrix products, arithmetic and copies ran while one was open for 1% of the time, Pallas kernels for 0%

commit v1 on v0

--- a/solution.py
+++ b/solution.py
@@ -33,7 +33,10 @@
             ).astype(jnp.bfloat16)
         )
     factor = jnp.concatenate(pieces, axis=1)
-    row_block = lax.all_gather(factor, "col", axis=0, tiled=True)
+    heap = []
+    for _ in range(lax.psum(1, "col")):
+        heap.append(factor)
+    row_block = jnp.concatenate(lax.all_to_all(jnp.stack(heap, axis=0), "col", 0, 0), 0)
     product = lax.dot_general(
         row_block,
         collect(factor, "row", 0),

time: 92.1 us -> 162 us (1.76)
  blocking collectives: 52.9 us -> 147 us
  between operations: 14 us -> 0.7 us
  waiting for transfers between devices: 6.57 us -> 0 us
  matrix products: 16.5 us -> 12.4 us
    all_to_all x0 -> x1, blocking collectives: none -> 94.2 us  [body(): lax.all_to_all(jnp.stack(heap, axis=0), 'col', 0, 0)]
    all_gather x1 -> x0, waiting for transfers between devices: 6.55 us -> none  [body(): row_block = lax.all_gather(factor, 'col', axis=0, tiled=True)]
    dot_general x1, matrix products: 13.8 us -> 9.72 us  [body(): lax.dot_general(row_block, collect(factor, 'row', 0), (((1,), (1,)), ((),...]
  transfers between devices with their start and end apart: 1 -> 0, of which waited for: 1 -> 0; matrix products, arithmetic and copies ran while one was open for 1% -> 0% of each run, Pallas kernels for 0% -> 0%
where the time goes in v1:
time: 162 us; the launch traced here: 161 us
  blocking collectives  147 us (91%)
  matrix products  12.4 us (8%)
    all_to_all x1, blocking collectives, body(): lax.all_to_all(jnp.stack(heap, axis=0), 'col', 0, 0)  94.2 us
    all_to_all x1, blocking collectives, sent_to_all(): lax.all_to_all(jnp.broadcast_to(x[None], (peers, *x.shape)), axis, 0, 0,...  52.9 us
    dot_general x1, matrix products, body(): lax.dot_general(row_block, collect(factor, 'row', 0), (((1,), (1,)), ((),...  9.72 us

profile of v1, /device:TPU:1, one launch (start us, length us, event | category | flops | bytes accessed | tf_op | source)
XLA Modules:
  0.0 161.4 jit_solution(9618058536714888133)
XLA Ops:
  0.6 1.3 fusion
  2.0 1.3 fusion.1
  3.3 0.0 copy-start
  3.4 0.2 broadcast_in_dim.12
  3.6 52.9 %all_to_all.10 = bf16[8,112,1024]{2,1,0:T(8,128)(2,1)S(1)} all-to-all(bf16[8,112,1024]{2,1,0:T(8,128)(2,1)S(1)} %broadcast_in_dim.12), channel_id=1, replica_groups=mesh['row'=8,'col'=32] {'row'}, dimensions={0} | all-to-all | bytes 3670016 | tf_op jit(solution)/shard_map/all_to_all | solution.py:12
  56.5 0.0 slice-start
  56.5 0.9 stack.2
  57.4 0.0 copy-done
  57.4 0.0 slice-start.1
  57.4 94.2 %all_to_all.11 = bf16[32,112,1024]{2,1,0:T(8,128)(2,1)S(1)} all-to-all(bf16[32,112,1024]{2,1,0:T(8,128)(2,1)S(1)} %stack.2), channel_id=1, replica_groups=mesh['row'=8,'col'=32] {'col'}, dimensions={0} | all-to-all | bytes 14680064 | tf_op jit(solution)/shard_map/all_to_all | solution.py:39
  151.6 0.0 slice-done
  151.6 0.0 slice-done.1
  151.6 9.7 %subtract_convert_fusion = bf16[3584,896]{1,0:T(8,128)(2,1)} fusion(bf16[3584,896]{1,0:T(8,128)(2,1)S(1)} %bitcast.21, bf16[3584,1024]{1,0:T(8,128)(2,1)S(1)} %bitcast.18, bf16[896,1024]{1,0:T(8,128)(2,1)S(1)} %bitcast.19), kind=kOutput, calls=%fused_computation | convolution fusion | flops 6586302464 | bytes 22020096 | tf_op jit(solution)/shard_map/dot_general | solution.py:40
  (2 shorter events, 0.0 us)
Async XLA Ops:
  3.3 54.1 %copy-start = (bf16[112,1024]{1,0:T(8,128)(2,1)}, bf16[112,1024]{1,0:T(8,128)(2,1)S(1)}, u32[]{:S(2)}) copy-start(bf16[112,1024]{1,0:T(8,128)(2,1)S(1)} %pad_maximum_fusion) | copy-start | bytes 688132
  56.5 95.2 %slice-start = ((s8[6422528]{0:T(1024)(128)(4,1)}), s8[4194304]{0:T(1024)(128)(4,1)S(1)}, s32[]{:S(2)}) async-start(s8[6422528]{0:T(1024)(128)(4,1)} %bitcast.20), calls=%async_computation.2 | async-start | bytes 8388608
  57.4 94.2 %slice-start.1 = ((s8[6422528]{0:T(1024)(128)(4,1)}), s8[2228224]{0:T(1024)(128)(4,1)S(1)}, s32[]{:S(2)}) async-start(s8[6422528]{0:T(1024)(128)(4,1)} %bitcast.20), calls=%async_computation.3 | async-start | bytes 4456448
